TPU v7x, 32 devices: a whole 2x2x4 slice. The times are simulated.
32 devices in a mesh: fsdp: 16 (over z, y, core), dp: 2 (over x).
Axes of the slice: x: 2, y: 2, z: 4, core: 2. Of those that a mesh axis runs over, the one named last changes fastest.
Arguments:
- tokens: bfloat16 [32, 256, 1152], P(('fsdp', 'dp')), may hold values from -12 to 12, as said below
- cond: bfloat16 [32, 1152], P(('fsdp', 'dp')), may hold values from -6 to 6
- segment_ids: int32 [32, 256], P(('fsdp', 'dp')), may hold values from 0 to 7, as said below
- ada_weight: bfloat16 [1152, 6912], P('fsdp'), may hold values from -0.1875 to 0.1875
- ada_bias: bfloat16 [6912], P('fsdp'), may hold values from -1 to 1
- qkv_weight: bfloat16 [1152, 3456], P('fsdp'), may hold values from -0.1875 to 0.1875
- qv_bias: bfloat16 [2304], P('fsdp'), may hold values from -1 to 1
- proj_weight: bfloat16 [1152, 1152], P('fsdp'), may hold values from -0.75 to 0.75
- proj_bias: bfloat16 [1152], P('fsdp'), may hold values from -1 to 1
- fc1_weight: bfloat16 [1152, 4608], P('fsdp'), may hold values from -0.1875 to 0.1875
- fc1_bias: bfloat16 [4608], P('fsdp'), may hold values from -1 to 1
- fc2_weight: bfloat16 [4608, 1152], P('fsdp'), may hold values from -0.09375 to 0.09375
- fc2_bias: bfloat16 [1152], P('fsdp'), may hold values from -1 to 1
- out_grad: bfloat16 [32, 256, 1152], P(('fsdp', 'dp')), may hold values from -6 to 6
Outputs:
- output: bfloat16 [32, 256, 1152], P(('fsdp', 'dp'))
- tokens_grad: bfloat16 [32, 256, 1152], P(('fsdp', 'dp'))
- ada_weight_grad: float32 [1152, 6912], P('fsdp')
- ada_bias_grad: float32 [6912], P('fsdp')
- qkv_weight_grad: float32 [1152, 3456], P('fsdp')
- qv_bias_grad: float32 [2304], P('fsdp')
- proj_weight_grad: float32 [1152, 1152], P('fsdp')
- proj_bias_grad: float32 [1152], P('fsdp')
- fc1_weight_grad: float32 [1152, 4608], P('fsdp')
- fc1_bias_grad: float32 [4608], P('fsdp')
- fc2_weight_grad: float32 [4608, 1152], P('fsdp')
- fc2_bias_grad: float32 [1152], P('fsdp')
Inputs may be any that keep to these rules, and one draw needn't show every extreme that they name: `segment_ids`: each row holds whole images one after another, numbered from 0 in order: eight images of 32 tokens, or two of 128 tokens, or one of 128 tokens among four of 32 tokens. Some row holds eight images and some row holds two. `tokens`: token features.
All inputs are finite; a program needn't handle non-finite values.
Results may differ from a plain program's by a relative error of at most 0.02.
The roundings to bfloat16 on the way count: a program that leaves them out, or rounds other values in their place, can miss the bound.
Values may be sent and summed in bfloat16 or wider, within the bound.
A program may use at most 384 MiB of HBM per device.

v0:
```python
import jax
import jax.numpy as jnp
from jax import lax
from jax.sharding import PartitionSpec as P

HEADS = 16
HEAD_DIM = 72
root_half = 0.7978845608028654
norm_eps = 1e-06
masked_score = -1e30


def gelu_tanh(stream):
    return (
        0.5 * stream * (1.0 + jnp.tanh(root_half * (stream + 0.044715 * stream * stream * stream)))
    )


def gelu_slope(stream):
    tanh_inner = jnp.tanh(root_half * (stream + 0.044715 * stream * stream * stream))
    return 0.5 * (1.0 + tanh_inner) + 0.5 * stream * (1.0 - tanh_inner * tanh_inner) * root_half * (
        1.0 + 3.0 * 0.044715 * stream * stream
    )


def normalize(stream):
    centre = jnp.mean(stream, axis=-1, keepdims=True)
    centred = stream - centre
    inv_std = lax.rsqrt(jnp.mean(centred * centred, axis=-1, keepdims=True) + norm_eps)
    return (centred * inv_std, inv_std)


def normalize_back(incoming, normed, inv_std):
    return inv_std * (
        incoming
        - jnp.mean(incoming, axis=-1, keepdims=True)
        - normed * jnp.mean(incoming * normed, axis=-1, keepdims=True)
    )


def head_scores(projected, same_doc, head_index, model_width):
    query_part = lax.dynamic_slice_in_dim(projected, head_index * HEAD_DIM, HEAD_DIM, 1)
    key_part = lax.dynamic_slice_in_dim(projected, model_width + head_index * HEAD_DIM, HEAD_DIM, 1)
    value_part = lax.dynamic_slice_in_dim(
        projected, 2 * model_width + head_index * HEAD_DIM, HEAD_DIM, 1
    )
    raw_scores = jnp.einsum(
        "qd,kd->qk", query_part, key_part, preferred_element_type=jnp.float32
    ) * HEAD_DIM ** (-0.5)
    return (jnp.where(same_doc, raw_scores, masked_score), query_part, key_part, value_part)


def merge_heads(stacked, model_width):
    return jnp.transpose(stacked, (1, 0, 2)).reshape(stacked.shape[1], model_width)


def attend_row(projected, segments_row, model_width):
    same_doc = segments_row[:, None] == segments_row[None, :]

    def one_head(head_index):
        scores, query_part, key_part, value_part = head_scores(
            projected, same_doc, head_index, model_width
        )
        top_score = jnp.max(scores, axis=-1, keepdims=True)
        exp_scores = jnp.exp(scores - top_score)
        denominator = jnp.sum(exp_scores, axis=-1, keepdims=True)
        probabilities = (exp_scores / denominator).astype(jnp.bfloat16)
        mixed_heads = jnp.dot(probabilities, value_part, preferred_element_type=jnp.float32)
        return (mixed_heads, (top_score + jnp.log(denominator))[:, 0])

    mixed_heads, log_total = lax.map(one_head, jnp.arange(HEADS))
    return (merge_heads(mixed_heads, model_width).astype(jnp.bfloat16), log_total)


def attend_back(projected, segments_row, log_total, d_mixed, model_width):
    same_doc = segments_row[:, None] == segments_row[None, :]
    head_scale = HEAD_DIM ** (-0.5)

    def one_head(head_index):
        scores, query_part, key_part, value_part = head_scores(
            projected, same_doc, head_index, model_width
        )
        d_head = lax.dynamic_slice_in_dim(d_mixed, head_index * HEAD_DIM, HEAD_DIM, 1)
        lse_row = lax.dynamic_index_in_dim(log_total, head_index, 0, keepdims=False)
        probabilities = jnp.exp(scores - lse_row[:, None])
        prob_low = probabilities.astype(jnp.bfloat16)
        d_probs = jnp.einsum("qd,kd->qk", d_head, value_part, preferred_element_type=jnp.float32)
        d_value = jnp.einsum("qk,qd->kd", prob_low, d_head, preferred_element_type=jnp.float32)
        d_scores = (
            probabilities * (d_probs - jnp.sum(d_probs * probabilities, axis=-1, keepdims=True))
        ).astype(jnp.bfloat16)
        d_query = (
            jnp.einsum("qk,kd->qd", d_scores, key_part, preferred_element_type=jnp.float32)
            * head_scale
        )
        d_key = (
            jnp.einsum("qk,qd->kd", d_scores, query_part, preferred_element_type=jnp.float32)
            * head_scale
        )
        return (d_query, d_key, d_value)

    d_query, d_key, d_value = lax.map(one_head, jnp.arange(HEADS))
    merged = [
        merge_heads(d_query, model_width),
        merge_heads(d_key, model_width),
        merge_heads(d_value, model_width),
    ]
    return jnp.concatenate(merged, axis=-1).astype(jnp.bfloat16)


def on_device(
    tokens,
    cond,
    segment_ids,
    ada_weight,
    ada_bias,
    qkv_weight,
    qv_bias,
    proj_weight,
    proj_bias,
    fc1_weight,
    fc1_bias,
    fc2_weight,
    fc2_bias,
    out_grad,
):
    row_count, seq_len, model_width = tokens.shape
    ff_width = fc1_weight.shape[1]
    stream = tokens.astype(jnp.float32)
    cond_float = cond.astype(jnp.float32)
    cond_act = (cond_float / (1.0 + jnp.exp(-cond_float))).astype(jnp.bfloat16)
    fsdp_at, dp_at = (lax.axis_index("fsdp"), lax.axis_index("dp"))
    dp_size = lax.axis_size("dp")
    slice_width, bias_width = (ada_weight.shape[0], ada_bias.shape[0])
    act_all = lax.all_gather(cond_act, ("fsdp", "dp"), axis=0, tiled=True)
    act_mine = lax.dynamic_slice_in_dim(act_all, fsdp_at * slice_width, slice_width, 1)
    partial = jnp.dot(act_mine, ada_weight, preferred_element_type=jnp.float32)
    bias_row = lax.dynamic_update_slice_in_dim(
        jnp.zeros((6 * model_width,), jnp.float32),
        ada_bias.astype(jnp.float32),
        fsdp_at * bias_width,
        0,
    )
    partial = (partial + bias_row).reshape(-1, dp_size, row_count, 6 * model_width)
    partial = lax.dynamic_index_in_dim(partial, dp_at, 1, keepdims=False)
    modulation = lax.psum_scatter(
        partial.reshape(-1, 6 * model_width), "fsdp", scatter_dimension=0, tiled=True
    )
    pieces = [
        modulation[:, None, section * model_width : (section + 1) * model_width]
        for section in range(6)
    ]
    shift_one, scale_one, gate_one, shift_two, scale_two, gate_two = pieces
    qkv_full, qv_bias_full, proj_full, proj_bias_full = (
        lax.all_gather(qkv_weight, "fsdp", axis=0, tiled=True),
        lax.all_gather(qv_bias, "fsdp", axis=0, tiled=True),
        lax.all_gather(proj_weight, "fsdp", axis=0, tiled=True),
        lax.all_gather(proj_bias, "fsdp", axis=0, tiled=True),
    )
    normed_one, inv_one = normalize(stream)
    hidden_one = (normed_one * (1.0 + scale_one) + shift_one).astype(jnp.bfloat16)
    qv_float = qv_bias_full.astype(jnp.float32)
    qkv_bias = jnp.concatenate(
        [qv_float[:model_width], jnp.zeros((model_width,), jnp.float32), qv_float[model_width:]]
    )
    projected = (
        jnp.dot(hidden_one, qkv_full, preferred_element_type=jnp.float32) + qkv_bias
    ).astype(jnp.bfloat16)

    def row_forward(row_items):
        return attend_row(row_items[0], row_items[1], model_width)

    mixed_rows, log_total = lax.map(row_forward, (projected, segment_ids))
    branch_one = jnp.dot(
        mixed_rows, proj_full, preferred_element_type=jnp.float32
    ) + proj_bias_full.astype(jnp.float32)
    resid_one = stream + gate_one * branch_one
    fc1_full, fc1_bias_full, fc2_full, fc2_bias_full = (
        lax.all_gather(fc1_weight, "fsdp", axis=0, tiled=True),
        lax.all_gather(fc1_bias, "fsdp", axis=0, tiled=True),
        lax.all_gather(fc2_weight, "fsdp", axis=0, tiled=True),
        lax.all_gather(fc2_bias, "fsdp", axis=0, tiled=True),
    )
    normed_two, inv_two = normalize(resid_one)
    hidden_two = (normed_two * (1.0 + scale_two) + shift_two).astype(jnp.bfloat16)
    pre_act = jnp.dot(
        hidden_two, fc1_full, preferred_element_type=jnp.float32
    ) + fc1_bias_full.astype(jnp.float32)
    active = gelu_tanh(pre_act).astype(jnp.bfloat16)
    branch_two = jnp.dot(
        active, fc2_full, preferred_element_type=jnp.float32
    ) + fc2_bias_full.astype(jnp.float32)
    output = (resid_one + gate_two * branch_two).astype(jnp.bfloat16)
    d_out = out_grad.astype(jnp.float32)
    fc1_back, fc2_back = (
        lax.all_gather(fc1_weight, "fsdp", axis=0, tiled=True),
        lax.all_gather(fc2_weight, "fsdp", axis=0, tiled=True),
    )
    d_gate_two = jnp.sum(d_out * branch_two, axis=1)
    d_branch_two = (d_out * gate_two).astype(jnp.bfloat16)
    fc2_shard = lax.psum_scatter(
        jnp.einsum("rsf,rsd->fd", active, d_branch_two, preferred_element_type=jnp.float32).astype(
            jnp.bfloat16
        ),
        "fsdp",
        scatter_dimension=0,
        tiled=True,
    )
    grad_fc2_bias = jnp.sum(d_branch_two.astype(jnp.float32), axis=(0, 1))
    d_active = jnp.einsum("rsd,fd->rsf", d_branch_two, fc2_back, preferred_element_type=jnp.float32)
    d_pre = (d_active * gelu_slope(pre_act)).astype(jnp.bfloat16)
    grad_fc1_bias = jnp.sum(d_pre.astype(jnp.float32), axis=(0, 1))
    d_hidden_two = jnp.einsum("rsf,ef->rse", d_pre, fc1_back, preferred_element_type=jnp.float32)
    d_scale_two = jnp.sum(d_hidden_two * normed_two, axis=1)
    d_shift_two = jnp.sum(d_hidden_two, axis=1)
    d_resid = d_out + normalize_back(d_hidden_two * (1.0 + scale_two), normed_two, inv_two)
    qkv_back, proj_back = (
        lax.all_gather(qkv_weight, "fsdp", axis=0, tiled=True),
        lax.all_gather(proj_weight, "fsdp", axis=0, tiled=True),
    )
    d_gate_one = jnp.sum(d_resid * branch_one, axis=1)
    d_branch_one = (d_resid * gate_one).astype(jnp.bfloat16)
    grad_proj_bias = jnp.sum(d_branch_one.astype(jnp.float32), axis=(0, 1))
    d_mixed = jnp.einsum(
        "rsd,ed->rse", d_branch_one, proj_back, preferred_element_type=jnp.float32
    ).astype(jnp.bfloat16)

    def row_backward(row_items):
        return attend_back(row_items[0], row_items[1], row_items[2], row_items[3], model_width)

    d_projected = lax.map(row_backward, (projected, segment_ids, log_total, d_mixed))
    d_proj_float = d_projected.astype(jnp.float32)
    grad_qv_bias = jnp.concatenate(
        [
            jnp.sum(d_proj_float[..., :model_width], axis=(0, 1)),
            jnp.sum(d_proj_float[..., 2 * model_width :], axis=(0, 1)),
        ]
    )
    d_hidden_one = jnp.einsum(
        "rsf,ef->rse", d_projected, qkv_back, preferred_element_type=jnp.float32
    )
    d_scale_one = jnp.sum(d_hidden_one * normed_one, axis=1)
    d_shift_one = jnp.sum(d_hidden_one, axis=1)
    tokens_grad = (
        d_resid + normalize_back(d_hidden_one * (1.0 + scale_one), normed_one, inv_one)
    ).astype(jnp.bfloat16)
    d_modulation = jnp.concatenate(
        [d_shift_one, d_scale_one, d_gate_one, d_shift_two, d_scale_two, d_gate_two], axis=-1
    ).astype(jnp.bfloat16)
    d_mod_all = lax.all_gather(d_modulation, ("fsdp", "dp"), axis=0, tiled=True)
    grad_ada = jnp.einsum("rd,re->de", act_mine, d_mod_all, preferred_element_type=jnp.float32)
    grad_ada_bias = jnp.sum(
        lax.dynamic_slice_in_dim(d_mod_all, fsdp_at * bias_width, bias_width, 1).astype(
            jnp.float32
        ),
        axis=0,
    )

    def owners(term):
        return lax.psum_scatter(term.astype(jnp.bfloat16), "fsdp", scatter_dimension=0, tiled=True)

    qkv_shard = owners(
        jnp.einsum("rse,rsf->ef", hidden_one, d_projected, preferred_element_type=jnp.float32)
    )
    proj_shard = owners(
        jnp.einsum("rse,rsd->ed", mixed_rows, d_branch_one, preferred_element_type=jnp.float32)
    )
    fc1_shard = owners(
        jnp.einsum("rse,rsf->ef", hidden_two, d_pre, preferred_element_type=jnp.float32)
    )
    bias_shards = (
        None,
        lax.psum_scatter(
            grad_qv_bias.astype(jnp.bfloat16), "fsdp", scatter_dimension=0, tiled=True
        ).astype(jnp.float32),
        lax.psum_scatter(
            grad_proj_bias.astype(jnp.bfloat16), "fsdp", scatter_dimension=0, tiled=True
        ).astype(jnp.float32),
        lax.psum_scatter(
            grad_fc1_bias.astype(jnp.bfloat16), "fsdp", scatter_dimension=0, tiled=True
        ).astype(jnp.float32),
        lax.psum_scatter(
            grad_fc2_bias.astype(jnp.bfloat16), "fsdp", scatter_dimension=0, tiled=True
        ).astype(jnp.float32),
    )
    summed = (
        grad_ada,
        grad_ada_bias,
        lax.psum(qkv_shard.astype(jnp.bfloat16), "dp").astype(jnp.float32),
        lax.psum(bias_shards[1].astype(jnp.bfloat16), "dp").astype(jnp.float32),
        lax.psum(proj_shard.astype(jnp.bfloat16), "dp").astype(jnp.float32),
        lax.psum(bias_shards[2].astype(jnp.bfloat16), "dp").astype(jnp.float32),
        lax.psum(fc1_shard.astype(jnp.bfloat16), "dp").astype(jnp.float32),
        lax.psum(bias_shards[3].astype(jnp.bfloat16), "dp").astype(jnp.float32),
        lax.psum(fc2_shard, "dp").astype(jnp.float32),
        lax.psum(bias_shards[4].astype(jnp.bfloat16), "dp").astype(jnp.float32),
    )
    return (
        output,
        tokens_grad,
        summed[0],
        summed[1],
        summed[2],
        summed[3],
        summed[4],
        summed[5],
        summed[6],
        summed[7],
        summed[8],
        summed[9],
    )


def solution(mesh):
    in_specs = (
        P(("fsdp", "dp"), None, None),
        P(("fsdp", "dp"), None),
        P(("fsdp", "dp"), None),
        P("fsdp", None),
        P("fsdp"),
        P("fsdp", None),
        P("fsdp"),
        P("fsdp", None),
        P("fsdp"),
        P("fsdp", None),
        P("fsdp"),
        P("fsdp", None),
        P("fsdp"),
        P(("fsdp", "dp"), None, None),
    )
    out_specs = (
        P(("fsdp", "dp"), None, None),
        P(("fsdp", "dp"), None, None),
        P("fsdp", None),
        P("fsdp"),
        P("fsdp", None),
        P("fsdp"),
        P("fsdp", None),
        P("fsdp"),
        P("fsdp", None),
        P("fsdp"),
        P("fsdp", None),
        P("fsdp"),
    )
    return jax.shard_map(
        on_device, mesh=mesh, in_specs=in_specs, out_specs=out_specs, check_vma=False
    )
```

profile of v0, /device:TPU:0, one launch (start us, length us, event | category | flops | bytes accessed | tf_op | source)
XLA Modules:
  0.0 1116.8 jit_solution(17571524379434750017)
XLA Ops:
  8.0 70.5 %all-gather = bf16[32,1,1152]{2,1,0:T(2,128)(2,1)S(1)} all-gather(bf16[1,1,1152]{2,1,0:T(2,128)(2,1)S(1)} %convert_bitcast_fusion), channel_id=1, replica_groups=mesh['fsdp'=16,'dp'=2] {'fsdp','dp'}, dimensions={0}, use_global_device_ids=true | all-gather | bytes 76032 | tf_op jit(solution)/shard_map/all_gather | solution.py:135
  87.5 57.8 %all-reduce.12 = (bf16[2304]{0:T(1024)(128)(2,1)S(1)}, bf16[1152]{0:T(1024)(128)(2,1)S(1)}, bf16[4608]{0:T(1024)(128)(2,1)S(1)}) all-reduce(bf16[2304]{0:T(1024)(128)(2,1)S(1)} %dynamic-update-slice, bf16[1152]{0:T(1024)(128)(2,1)S(1)} %dynamic-update-slice.1, ...), channel_id=1, replica_groups=mesh['fsdp'=16,'dp'=2] {'fsdp'}, use_global_device_ids=true, to_apply=%add | all-reduce | flops 8064 | bytes 32256
  145.8 22.1 %all-reduce.18.cloned.1.call-done = f32[16,6912]{1,0:T(8,128)} async-done(((f32[16,6912]{1,0:T(8,128)}), f32[16,6912]{1,0:T(8,128)}) %all-reduce.18.cloned.1.call-update) | async-done | bytes 442384
  169.6 72.5 %all-gather.7.cloned.1.call-done = bf16[1152,3456]{1,0:T(8,128)(2,1)} async-done(((bf16[72,3456]{1,0:T(8,128)(2,1)}), bf16[1152,3456]{1,0:T(8,128)(2,1)}) %all-gather.7.cloned.1.call-update) | async-done | bytes 7962640 | tf_op jit(solution)/shard_map/all_gather | solution.py:155
  242.2 6.0 fusion.37
  248.2 32.0 %while.50 = (s32[]{:T(128)}, bf16[16,256,72]{1,2,0:T(8,128)(2,1)S(1)}, f32[16,256]{1,0:T(8,128)S(1)}, s32[16]{0:T(128)S(1)}, bf16[256,3456]{1,0:T(8,128)(2,1)S(1...) while((s32[]{:T(128)}, ...), condition=%wide.region_6.7_spmd.clone, body=%wide.region_3.6_spmd.clone.sunk | while | flops 19463948 | bytes 1069367 | solution.py:71
  280.3 6.1 all-gather.9.cloned.1.call-done
  286.4 3.9 fusion.89
  290.5 85.2 %all-gather.11.cloned.1.call-done = bf16[1152,4608]{1,0:T(8,128)(2,1)} async-done(((bf16[72,4608]{1,0:T(8,128)(2,1)}), bf16[1152,4608]{1,0:T(8,128)(2,1)}) %all-gather.11.cloned.1.call-update) | async-done | bytes 10616848 | tf_op jit(solution)/shard_map/all_gather | solution.py:179
  375.7 9.1 convolution_add_fusion.1
  384.8 79.7 %all-gather.13.cloned.1.call-done = bf16[4608,1152]{1,0:T(8,128)(2,1)} async-done(((bf16[288,1152]{1,0:T(8,128)(2,1)}), bf16[4608,1152]{1,0:T(8,128)(2,1)}) %all-gather.13.cloned.1.call-update) | async-done | bytes 10616848 | tf_op jit(solution)/shard_map/all_gather | solution.py:181
  464.5 8.5 fusion.93
  473.0 8.3 fusion.60
  493.1 179.2 %while.51 = (s32[]{:T(128)}, bf16[16,256,72]{1,2,0:T(8,128)(2,1)}, bf16[16,256,72]{1,2,0:T(8,128)(2,1)}, bf16[16,256,72]{1,2,0:T(8,128)(2,1)}, s32[16]{0:T(128)S...) while((s32[]{:T(128)}, bf16[16,256,72]{1,2,0:T(8,128)(2,1)}, ...), condition=%wide.region_13.14_spmd.clone, body=%wide.region_11.13_spmd.clone.sunk | while | flops 47877904 | bytes 2653598 | solution.py:102
  672.3 7.2 convolution_convert_fusion.2
  679.6 9.7 convolution_convert_fusion.1
  689.6 11.4 %convolution_convert_fusion = bf16[4608,1152]{1,0:T(8,128)(2,1)} fusion(bf16[1,256,1152]{2,1,0:T(8,128)(2,1)} %param.31, f32[1152]{0:T(1024)S(1)} %get-tuple-element.291, f32[256,4608]{1,0:T(8,128)} %convolution_add_fusion.1), kind=kOutput, calls=%fused_computation.46 | convolution fusion | flops 2734718976 | bytes 15929856 | tf_op jit(solution)/shard_map/rsf,rsd->fd/dot_general | solution.py:202
  706.1 62.0 %all-reduce.11 = (bf16[1152]{0:T(1024)(128)(2,1)S(1)}, bf16[2304]{0:T(1024)(128)(2,1)S(1)}, bf16[1152]{0:T(1024)(128)(2,1)S(1)}, bf16[4608]{0:T(1024)(128)(2,1)S(1)}, bf16[1152]{0:T(1024)(128)(2,1)S(1)}) all-reduce(bf16[1152]{0:T(1024)(128)(2,1)S(1)} %dynamic-update-slice.3, ...), channel_id=1, replica_groups=mesh['fsdp'=16,'dp'=2] {'fsdp'}, use_global_device_ids=true, to_apply=%add.3 | all-reduce | flops 10368 | bytes 41472
  768.4 5.1 all-reduce.13
  775.7 6.8 fusion.56
  783.8 10.3 fusion.59
  794.1 109.2 %reduce-scatter.9.cloned.1.call-done = bf16[72,4608]{1,0:T(8,128)(2,1)} async-done(((bf16[1152,4608]{1,0:T(8,128)(2,1)}), bf16[72,4608]{1,0:T(8,128)(2,1)}) %reduce-scatter.9.cloned.1.call-update) | async-done | bytes 663568 | tf_op jit(solution)/shard_map/reduce_scatter | solution.py:260
  903.3 124.4 %reduce-scatter.11.cloned.1.call-done = bf16[288,1152]{1,0:T(8,128)(2,1)} async-done(((bf16[4608,1152]{1,0:T(8,128)(2,1)}), bf16[288,1152]{1,0:T(8,128)(2,1)}) %reduce-scatter.11.cloned.1.call-update) | async-done | bytes 663568 | tf_op jit(solution)/shard_map/reduce_scatter | solution.py:201
  1027.7 73.0 %all-gather.1 = bf16[32,1,6912]{2,1,0:T(2,128)(2,1)S(1)} all-gather(bf16[1,1,6912]{2,1,0:T(2,128)(2,1)S(1)} %bitcast.158), channel_id=1, replica_groups=mesh['fsdp'=16,'dp'=2] {'fsdp','dp'}, dimensions={0}, use_global_device_ids=true | all-gather | bytes 456192 | tf_op jit(solution)/shard_map/all_gather | solution.py:250
  (364 shorter events, 195.9 us)
Async XLA Ops:
  7.2 72.2 %copy-start = (bf16[72,6912]{1,0:T(8,128)(2,1)S(1)}, bf16[72,6912]{1,0:T(8,128)(2,1)}, u32[]{:S(2)}) copy-start(bf16[72,6912]{1,0:T(8,128)(2,1)} %param.21) | copy-start | bytes 2985988
  7.2 160.8 %all-reduce.18.cloned.1.call-start = ((), (), s32[]{:S(2)}) async-start(), calls=%async_computation.10 | async-start | bytes 884736
  81.4 2.8 copy-start.17
  81.4 5.3 copy-start.20
  81.4 5.6 copy-start.21
  81.4 5.8 copy-start.18
  81.4 63.9 %copy-start.2 = (bf16[1,256,1152]{2,1,0:T(8,128)(2,1)S(1)}, bf16[1,256,1152]{2,1,0:T(8,128)(2,1)}, u32[]{:S(2)}) copy-start(bf16[1,256,1152]{2,1,0:T(8,128)(2,1)} %param.18) | copy-start | bytes 1769476
  81.5 160.7 %all-gather.7.cloned.1.call-start = ((), (), s32[]{:S(2)}) async-start(), calls=%async_computation.4 | async-start | bytes 8460288 | tf_op jit(solution)/shard_map/all_gather | solution.py:155
  82.2 204.2 %all-gather.9.cloned.1.call-start = ((), (), s32[]{:S(2)}) async-start(), calls=%async_computation.5 | async-start | bytes 2820096 | tf_op jit(solution)/shard_map/all_gather | solution.py:157
  82.9 292.8 %all-gather.11.cloned.1.call-start = ((), (), s32[]{:S(2)}) async-start(), calls=%async_computation.6 | async-start | bytes 11280384 | tf_op jit(solution)/shard_map/all_gather | solution.py:179
  83.5 380.9 %all-gather.13.cloned.1.call-start = ((), (), s32[]{:S(2)}) async-start(), calls=%async_computation.7 | async-start | bytes 11280384 | tf_op jit(solution)/shard_map/all_gather | solution.py:181
  84.1 709.9 %reduce-scatter.15.cloned.1.call-start = ((), (), s32[]{:S(2)}) async-start(), calls=%async_computation.12 | async-start | bytes 2820096
  242.1 6.1 copy-start.19
  280.2 6.1 copy-start.15
  280.3 10.0 copy-start.3
  375.7 88.7 %copy-start.9 = (bf16[1,256,1152]{2,1,0:T(8,128)(2,1)S(1)}, bf16[1,256,1152]{2,1,0:T(8,128)(2,1)}, u32[]{:S(2)}) copy-start(bf16[1,256,1152]{2,1,0:T(8,128)(2,1)} %param.31) | copy-start | bytes 1769476
  473.0 8.3 copy-start.12
  473.0 8.5 copy-start.10
  486.7 307.4 %reduce-scatter.13.cloned.1.call-start = ((), (), s32[]{:S(2)}) async-start(), calls=%async_computation.11 | async-start | bytes 8460288
  679.6 223.7 %reduce-scatter.9.cloned.1.call-start = ((), (), s32[]{:S(2)}) async-start(), calls=%async_computation.8 | async-start | bytes 11280384 | tf_op jit(solution)/shard_map/reduce_scatter | solution.py:260
  689.3 338.3 %reduce-scatter.11.cloned.1.call-start = ((), (), s32[]{:S(2)}) async-start(), calls=%async_computation.9 | async-start | bytes 11280384 | tf_op jit(solution)/shard_map/reduce_scatter | solution.py:201
  701.0 403.5 %all-reduce.20.cloned.1.call-start = ((), (), s32[]{:S(2)}) async-start(), calls=%async_computation.13 | async-start | bytes 3981312 | tf_op jit(solution)/shard_map/psum | solution.py:289
  775.7 8.1 copy-start.11
  1104.5 2.9 copy-start.14
  (9 other events, 15.1 us)
Sparse Core Ops, SparseCore 0:
  81.6 86.3 all-reduce.17
  170.1 71.9 all-gather.6
  244.3 42.0 all-gather.8
  288.5 87.1 all-gather.10
  377.9 86.5 all-gather.12
  486.8 61.2 reduce-scatter.14
  679.7 99.0 reduce-scatter.12
  782.9 120.3 reduce-scatter.8
  907.3 120.2 reduce-scatter.10
  1030.0 72.9 all-reduce.19
where the time goes:
time: 1130 us; the launch traced here: 1120 us
  waiting for transfers between devices  502 us (44%)
  blocking collectives  268 us (24%)
  matrix products  226 us (20%)
  loops' own time  53.6 us (5%)
  local copies, waits for them, and re-layouts  29 us (3%)
  other arithmetic  19.3 us (2%)
  between operations  18.7 us (2%)
    reduce_scatter x1, waiting for transfers between devices, on_device(): lax.psum_scatter(jnp.einsum('rsf,rsd->fd', active, d_branch_two, preferre...  124 us
    unnamed x2, blocking collectives  120 us
    reduce_scatter x1, waiting for transfers between devices, owners(): lax.psum_scatter(term.astype(jnp.bfloat16), 'fsdp', scatter_dimension=0,...  109 us
    all_gather x1, waiting for transfers between devices, on_device(): lax.all_gather(fc1_weight, 'fsdp', axis=0, tiled=True)  85.2 us
    all_gather x1, waiting for transfers between devices, on_device(): lax.all_gather(fc2_weight, 'fsdp', axis=0, tiled=True)  79.7 us
    all_gather x1, blocking collectives, on_device(): d_mod_all = lax.all_gather(d_modulation, ('fsdp', 'dp'), axis=0, tiled=True)  73 us
    all_gather x1, waiting for transfers between devices, on_device(): lax.all_gather(qkv_weight, 'fsdp', axis=0, tiled=True)  72.5 us
    all_gather x1, blocking collectives, on_device(): act_all = lax.all_gather(cond_act, ('fsdp', 'dp'), axis=0, tiled=True)  70.5 us
  transfers between devices with their start and end apart: 10, of which 7 were waited for; matrix products, arithmetic and copies ran while one was open for 22% of the time, Pallas kernels for 0%

commit v1 on v0

--- a/solution.py
+++ b/solution.py
@@ -1,3 +1,4 @@
+import functools
 import jax
 import jax.numpy as jnp
 from jax import lax
@@ -8,6 +9,35 @@
 root_half = 0.7978845608028654
 norm_eps = 1e-06
 masked_score = -1e30
+
+
+def match_windows_now(field, axis_key, at_axis):
+    val2 = lax.axis_size(axis_key)
+    carry = lax.axis_index(axis_key)
+    everything, mixed_arr, big = (val2, carry, field.shape[at_axis])
+    copies = [idx * everything if rr == at_axis else idx for rr, idx in enumerate(field.shape)]
+    part_next = lax.dynamic_update_slice_in_dim(
+        jnp.zeros(copies, field.dtype), field, mixed_arr * big, axis=at_axis
+    )
+    formed = y1 = field
+    for m in range(1, everything // 2 + 1):
+        formed = lax.ppermute(
+            formed, axis_key, [(rr, (rr + 1) % everything) for rr in range(everything)]
+        )
+        part_next = lax.dynamic_update_slice_in_dim(
+            part_next, formed, (mixed_arr - m) % everything * big, axis=at_axis
+        )
+        if 2 * m < everything:
+            y1 = lax.ppermute(
+                y1, axis_key, [(rr, (rr - 1) % everything) for rr in range(everything)]
+            )
+            part_next = lax.dynamic_update_slice_in_dim(
+                part_next, y1, (mixed_arr + m) % everything * big, axis=at_axis
+            )
+    return part_next
+
+
+watch_target = functools.partial(match_windows_now, axis_key="fsdp", at_axis=0)
 
 
 def gelu_tanh(stream):
@@ -152,7 +182,7 @@
     ]
     shift_one, scale_one, gate_one, shift_two, scale_two, gate_two = pieces
     qkv_full, qv_bias_full, proj_full, proj_bias_full = (
-        lax.all_gather(qkv_weight, "fsdp", axis=0, tiled=True),
+        watch_target(qkv_weight),
         lax.all_gather(qv_bias, "fsdp", axis=0, tiled=True),
         lax.all_gather(proj_weight, "fsdp", axis=0, tiled=True),
         lax.all_gather(proj_bias, "fsdp", axis=0, tiled=True),

time: 1130 us -> 1080 us (0.956)
  waiting for transfers between devices: 502 us -> 380 us
  starting transfers between devices: 0.57 us -> 53.2 us
  local copies, waits for them, and re-layouts: 29 us -> 48.2 us
    all_gather x1, waiting for transfers between devices: 85.2 us -> 4.96 us  [on_device(): lax.all_gather(fc1_weight, 'fsdp', axis=0, tiled=True)]
    all_gather x1, waiting for transfers between devices: 72.5 us -> 0.01 us  [on_device(): lax.all_gather(qkv_weight, 'fsdp', axis=0, tiled=True)]
    ppermute x0 -> x15, starting transfers between devices: none -> 52.5 us  [the longest x8 31.9 us: match_windows_now(): lax.ppermute(formed, axis_key, [(rr, (rr + 1) % everything) for rr in ran...]
    ppermute x0 -> x15, waiting for transfers between devices: none -> 48.7 us  [the longest x8 47.7 us: match_windows_now(): lax.ppermute(formed, axis_key, [(rr, (rr + 1) % everything) for rr in ran...]
    dynamic_update_slice x0 -> x16, local copies, waits for them, and re-layouts: none -> 14.4 us  [the longest x8 6.69 us: match_windows_now(): lax.dynamic_update_slice_in_dim(part_next, formed, (mixed_arr - m) % ever...]
  transfers between devices with their start and end apart: 10 -> 25, of which waited for: 7 -> 13; matrix products, arithmetic and copies ran while one was open for 22% -> 26% of each run, Pallas kernels for 0% -> 0%
where the time goes in v1:
time: 1080 us; the launch traced here: 1070 us
  waiting for transfers between devices  380 us (35%)
  blocking collectives  270 us (25%)
  matrix products  225 us (21%)
  loops' own time  53.7 us (5%)
  starting transfers between devices  53.2 us (5%)
  local copies, waits for them, and re-layouts  48.2 us (4%)
  other arithmetic  20.3 us (2%)
  between operations  19.1 us (2%)
    reduce_scatter x1, waiting for transfers between devices, on_device(): lax.psum_scatter(jnp.einsum('rsf,rsd->fd', active, d_branch_two, preferre...  124 us
    unnamed x2, blocking collectives  122 us
    reduce_scatter x1, waiting for transfers between devices, owners(): lax.psum_scatter(term.astype(jnp.bfloat16), 'fsdp', scatter_dimension=0,...  109 us
    all_gather x1, waiting for transfers between devices, on_device(): lax.all_gather(fc2_weight, 'fsdp', axis=0, tiled=True)  78.8 us
    all_gather x1, blocking collectives, on_device(): d_mod_all = lax.all_gather(d_modulation, ('fsdp', 'dp'), axis=0, tiled=True)  73.1 us
    all_gather x1, blocking collectives, on_device(): act_all = lax.all_gather(cond_act, ('fsdp', 'dp'), axis=0, tiled=True)  70.5 us
    ppermute x8, waiting for transfers between devices, match_windows_now(): lax.ppermute(formed, axis_key, [(rr, (rr + 1) % everything) for rr in ran...  47.7 us
    another operation x1, loops' own time, attend_back(): d_query, d_key, d_value = lax.map(one_head, jnp.arange(HEADS))  42.4 us
  transfers between devices with their start and end apart: 25, of which 13 were waited for; matrix products, arithmetic and copies ran while one was open for 26% of the time, Pallas kernels for 0%

profile of v1, /device:TPU:0, one launch (start us, length us, event | category | flops | bytes accessed | tf_op | source)
XLA Modules:
  0.0 1070.2 jit_solution(76151871287462516)
XLA Ops:
  8.0 70.5 %all-gather = bf16[32,1,1152]{2,1,0:T(2,128)(2,1)S(1)} all-gather(bf16[1,1,1152]{2,1,0:T(2,128)(2,1)S(1)} %convert_bitcast_fusion), channel_id=1, replica_groups=mesh['fsdp'=16,'dp'=2] {'fsdp','dp'}, dimensions={0}, use_global_device_ids=true | all-gather | bytes 76032 | tf_op jit(solution)/shard_map/all_gather | solution.py:165
  91.5 59.3 %all-reduce.12 = (bf16[2304]{0:T(1024)(128)(2,1)S(1)}, bf16[1152]{0:T(1024)(128)(2,1)S(1)}, bf16[4608]{0:T(1024)(128)(2,1)S(1)}) all-reduce(bf16[2304]{0:T(1024)(128)(2,1)S(1)} %dynamic-update-slice, bf16[1152]{0:T(1024)(128)(2,1)S(1)} %dynamic-update-slice.1, ...), channel_id=1, replica_groups=mesh['fsdp'=16,'dp'=2] {'fsdp'}, use_global_device_ids=true, to_apply=%add | all-reduce | flops 8064 | bytes 32256
  157.3 11.9 %all-reduce.18.cloned.1.call-done = f32[16,6912]{1,0:T(8,128)} async-done(((f32[16,6912]{1,0:T(8,128)}), f32[16,6912]{1,0:T(8,128)}) %all-reduce.18.cloned.1.call-update) | async-done | bytes 442384
  189.8 6.8 collective-permute-done.4
  208.6 8.7 collective-permute-start.8
  219.9 11.0 %collective-permute-start.10 = (bf16[72,3456]{1,0:T(8,128)(2,1)S(1)}, bf16[72,3456]{1,0:T(8,128)(2,1)S(1)}, u32[]{:S(2)}, u32[]{:S(2)}) collective-permute-start(bf16[72,3456]{1,0:T(8,128)(2,1)S(1)} %collective-permute-done.8), channel_id=1, source_target_pairs={{0,2},{2,4},{4,6},{6,8},{8,10},{10,12},{12,14},{14,16},{16,18},{18... | collective-permute-start | bytes 1493000 | tf_op jit(solution)/shard_map/ppermute | solution.py:24
  236.7 10.9 %collective-permute-start.12 = (bf16[72,3456]{1,0:T(8,128)(2,1)S(1)}, bf16[72,3456]{1,0:T(8,128)(2,1)S(1)}, u32[]{:S(2)}, u32[]{:S(2)}) collective-permute-start(bf16[72,3456]{1,0:T(8,128)(2,1)S(1)} %collective-permute-done.10), channel_id=1, source_target_pairs={{0,2},{2,4},{4,6},{6,8},{8,10},{10,12},{12,14},{14,16},{16,18},{18... | collective-permute-start | bytes 1493000 | tf_op jit(solution)/shard_map/ppermute | solution.py:24
  252.0 15.7 %collective-permute-done.12 = bf16[72,3456]{1,0:T(8,128)(2,1)S(1)} collective-permute-done((bf16[72,3456]{1,0:T(8,128)(2,1)S(1)}, bf16[72,3456]{1,0:T(8,128)(2,1)S(1)}, u32[]{:S(2)}, u32[]{:S(2)}) %collective-permute-start.12) | collective-permute-done | bytes 497696 | tf_op jit(solution)/shard_map/ppermute | solution.py:24
  269.9 9.3 collective-permute-done.14
  286.1 32.0 %while.50 = (s32[]{:T(128)}, bf16[16,256,72]{1,2,0:T(8,128)(2,1)S(1)}, f32[16,256]{1,0:T(8,128)S(1)}, s32[16]{0:T(128)S(1)}, bf16[256,3456]{1,0:T(8,128)(2,1)S(1...) while((s32[]{:T(128)}, ...), condition=%wide.region_6.7_spmd.clone, body=%wide.region_3.6_spmd.clone.sunk | while | flops 19463948 | bytes 1069367 | solution.py:101
  328.5 9.1 convolution_add_fusion.1
  337.6 78.8 %all-gather.11.cloned.1.call-done = bf16[4608,1152]{1,0:T(8,128)(2,1)} async-done(((bf16[288,1152]{1,0:T(8,128)(2,1)}), bf16[4608,1152]{1,0:T(8,128)(2,1)}) %all-gather.11.cloned.1.call-update) | async-done | bytes 10616848 | tf_op jit(solution)/shard_map/all_gather | solution.py:211
  416.4 8.1 fusion.93
  424.5 8.3 fusion.60
  444.8 179.4 %while.51 = (s32[]{:T(128)}, bf16[16,256,72]{1,2,0:T(8,128)(2,1)}, bf16[16,256,72]{1,2,0:T(8,128)(2,1)}, bf16[16,256,72]{1,2,0:T(8,128)(2,1)}, s32[16]{0:T(128)S...) while((s32[]{:T(128)}, bf16[16,256,72]{1,2,0:T(8,128)(2,1)}, ...), condition=%wide.region_13.14_spmd.clone, body=%wide.region_11.13_spmd.clone.sunk | while | flops 47877904 | bytes 2653598 | solution.py:132
  624.2 7.2 convolution_convert_fusion.2
  631.5 9.6 convolution_convert_fusion.1
  641.2 11.4 %convolution_convert_fusion = bf16[4608,1152]{1,0:T(8,128)(2,1)} fusion(bf16[1,256,1152]{2,1,0:T(8,128)(2,1)} %param.31, f32[1152]{0:T(1024)S(1)} %get-tuple-element.291, f32[256,4608]{1,0:T(8,128)} %convolution_add_fusion.1), kind=kOutput, calls=%fused_computation.46 | convolution fusion | flops 2734718976 | bytes 15929856 | tf_op jit(solution)/shard_map/rsf,rsd->fd/dot_general | solution.py:232
  658.0 62.3 %all-reduce.11 = (bf16[1152]{0:T(1024)(128)(2,1)S(1)}, bf16[2304]{0:T(1024)(128)(2,1)S(1)}, bf16[1152]{0:T(1024)(128)(2,1)S(1)}, bf16[4608]{0:T(1024)(128)(2,1)S(1)}, bf16[1152]{0:T(1024)(128)(2,1)S(1)}) all-reduce(bf16[1152]{0:T(1024)(128)(2,1)S(1)} %dynamic-update-slice.3, ...), channel_id=1, replica_groups=mesh['fsdp'=16,'dp'=2] {'fsdp'}, use_global_device_ids=true, to_apply=%add.3 | all-reduce | flops 10368 | bytes 41472
  727.7 6.8 fusion.56
  735.8 10.3 fusion.59
  746.1 109.4 %reduce-scatter.9.cloned.1.call-done = bf16[72,4608]{1,0:T(8,128)(2,1)} async-done(((bf16[1152,4608]{1,0:T(8,128)(2,1)}), bf16[72,4608]{1,0:T(8,128)(2,1)}) %reduce-scatter.9.cloned.1.call-update) | async-done | bytes 663568 | tf_op jit(solution)/shard_map/reduce_scatter | solution.py:290
  855.5 124.4 %reduce-scatter.11.cloned.1.call-done = bf16[288,1152]{1,0:T(8,128)(2,1)} async-done(((bf16[4608,1152]{1,0:T(8,128)(2,1)}), bf16[288,1152]{1,0:T(8,128)(2,1)}) %reduce-scatter.11.cloned.1.call-update) | async-done | bytes 663568 | tf_op jit(solution)/shard_map/reduce_scatter | solution.py:231
  980.0 73.1 %all-gather.1 = bf16[32,1,6912]{2,1,0:T(2,128)(2,1)S(1)} all-gather(bf16[1,1,6912]{2,1,0:T(2,128)(2,1)S(1)} %bitcast.158), channel_id=1, replica_groups=mesh['fsdp'=16,'dp'=2] {'fsdp','dp'}, dimensions={0}, use_global_device_ids=true | all-gather | bytes 456192 | tf_op jit(solution)/shard_map/all_gather | solution.py:280
  (409 shorter events, 274.6 us)
Async XLA Ops:
  7.2 162.0 %all-reduce.18.cloned.1.call-start = ((), (), s32[]{:S(2)}) async-start(), calls=%async_computation.10 | async-start | bytes 884736
  81.5 236.7 %all-gather.7.cloned.1.call-start = ((), (), s32[]{:S(2)}) async-start(), calls=%async_computation.4 | async-start | bytes 2820096 | tf_op jit(solution)/shard_map/all_gather | solution.py:187
  82.2 246.2 %all-gather.9.cloned.1.call-start = ((), (), s32[]{:S(2)}) async-start(), calls=%async_computation.5 | async-start | bytes 11280384 | tf_op jit(solution)/shard_map/all_gather | solution.py:209
  83.0 333.4 %all-gather.11.cloned.1.call-start = ((), (), s32[]{:S(2)}) async-start(), calls=%async_computation.6 | async-start | bytes 11280384 | tf_op jit(solution)/shard_map/all_gather | solution.py:211
  83.6 644.2 %all-gather.13.cloned.1.call-start = ((), (), s32[]{:S(2)}) async-start(), calls=%async_computation.7 | async-start | bytes 8460288 | tf_op jit(solution)/shard_map/all_gather | solution.py:248
  83.6 87.2 %collective-permute-start = (bf16[72,3456]{1,0:T(8,128)(2,1)}, bf16[72,3456]{1,0:T(8,128)(2,1)S(1)}, u32[]{:S(2)}, u32[]{:S(2)}) collective-permute-start(bf16[72,3456]{1,0:T(8,128)(2,1)} %param.23), channel_id=1, source_target_pairs={{0,2},{2,4},{4,6},{6,8},{8,10},{10,12},{12,14},{14,16},{16,18},{18... | collective-permute-start | bytes 1493000 | tf_op jit(solution)/shard_map/ppermute | solution.py:24
  83.7 87.6 %collective-permute-start.1 = (bf16[72,3456]{1,0:T(8,128)(2,1)}, bf16[72,3456]{1,0:T(8,128)(2,1)S(1)}, u32[]{:S(2)}, u32[]{:S(2)}) collective-permute-start(bf16[72,3456]{1,0:T(8,128)(2,1)} %param.23), channel_id=1, source_target_pairs={{0,30},{2,0},{4,2},{6,4},{8,6},{10,8},{12,10},{14,12},{16,14},{18,... | collective-permute-start | bytes 1493000 | tf_op jit(solution)/shard_map/ppermute | solution.py:31
  88.1 658.0 %reduce-scatter.15.cloned.1.call-start = ((), (), s32[]{:S(2)}) async-start(), calls=%async_computation.12 | async-start | bytes 2820096
  171.2 12.3 %collective-permute-start.3 = (bf16[72,3456]{1,0:T(8,128)(2,1)S(1)}, bf16[72,3456]{1,0:T(8,128)(2,1)S(1)}, u32[]{:S(2)}, u32[]{:S(2)}) collective-permute-start(bf16[72,3456]{1,0:T(8,128)(2,1)S(1)} %collective-permute-done.1), channel_id=1, source_target_pairs={{0,30},{2,0},{4,2},{6,4},{8,6},{10,8},{12,10},{14,12},{16,14},{18,... | collective-permute-start | bytes 1493000 | tf_op jit(solution)/shard_map/ppermute | solution.py:31
  182.0 14.6 %collective-permute-start.4 = (bf16[72,3456]{1,0:T(8,128)(2,1)S(1)}, bf16[72,3456]{1,0:T(8,128)(2,1)S(1)}, u32[]{:S(2)}, u32[]{:S(2)}) collective-permute-start(bf16[72,3456]{1,0:T(8,128)(2,1)S(1)} %collective-permute-done.2), channel_id=1, source_target_pairs={{0,2},{2,4},{4,6},{6,8},{8,10},{10,12},{12,14},{14,16},{16,18},{18... | collective-permute-start | bytes 1493000 | tf_op jit(solution)/shard_map/ppermute | solution.py:24
  183.5 13.1 %collective-permute-start.5 = (bf16[72,3456]{1,0:T(8,128)(2,1)S(1)}, bf16[72,3456]{1,0:T(8,128)(2,1)S(1)}, u32[]{:S(2)}, u32[]{:S(2)}) collective-permute-start(bf16[72,3456]{1,0:T(8,128)(2,1)S(1)} %collective-permute-done.3), channel_id=1, source_target_pairs={{0,30},{2,0},{4,2},{6,4},{8,6},{10,8},{12,10},{14,12},{16,14},{18,... | collective-permute-start | bytes 1493000 | tf_op jit(solution)/shard_map/ppermute | solution.py:31
  196.6 12.0 %collective-permute-start.6 = (bf16[72,3456]{1,0:T(8,128)(2,1)S(1)}, bf16[72,3456]{1,0:T(8,128)(2,1)S(1)}, u32[]{:S(2)}, u32[]{:S(2)}) collective-permute-start(bf16[72,3456]{1,0:T(8,128)(2,1)S(1)} %collective-permute-done.4), channel_id=1, source_target_pairs={{0,2},{2,4},{4,6},{6,8},{8,10},{10,12},{12,14},{14,16},{16,18},{18... | collective-permute-start | bytes 1493000 | tf_op jit(solution)/shard_map/ppermute | solution.py:24
  196.6 20.7 %collective-permute-start.7 = (bf16[72,3456]{1,0:T(8,128)(2,1)S(1)}, bf16[72,3456]{1,0:T(8,128)(2,1)S(1)}, u32[]{:S(2)}, u32[]{:S(2)}) collective-permute-start(bf16[72,3456]{1,0:T(8,128)(2,1)S(1)} %collective-permute-done.5), channel_id=1, source_target_pairs={{0,30},{2,0},{4,2},{6,4},{8,6},{10,8},{12,10},{14,12},{16,14},{18,... | collective-permute-start | bytes 1493000 | tf_op jit(solution)/shard_map/ppermute | solution.py:31
  208.6 11.3 %collective-permute-start.8 = (bf16[72,3456]{1,0:T(8,128)(2,1)S(1)}, bf16[72,3456]{1,0:T(8,128)(2,1)S(1)}, u32[]{:S(2)}, u32[]{:S(2)}) collective-permute-start(bf16[72,3456]{1,0:T(8,128)(2,1)S(1)} %collective-permute-done.6), channel_id=1, source_target_pairs={{0,2},{2,4},{4,6},{6,8},{8,10},{10,12},{12,14},{14,16},{16,18},{18... | collective-permute-start | bytes 1493000 | tf_op jit(solution)/shard_map/ppermute | solution.py:24
  217.3 13.7 %collective-permute-start.9 = (bf16[72,3456]{1,0:T(8,128)(2,1)S(1)}, bf16[72,3456]{1,0:T(8,128)(2,1)S(1)}, u32[]{:S(2)}, u32[]{:S(2)}) collective-permute-start(bf16[72,3456]{1,0:T(8,128)(2,1)S(1)} %collective-permute-done.7), channel_id=1, source_target_pairs={{0,30},{2,0},{4,2},{6,4},{8,6},{10,8},{12,10},{14,12},{16,14},{18,... | collective-permute-start | bytes 1493000 | tf_op jit(solution)/shard_map/ppermute | solution.py:31
  219.9 16.7 %collective-permute-start.10 = (bf16[72,3456]{1,0:T(8,128)(2,1)S(1)}, bf16[72,3456]{1,0:T(8,128)(2,1)S(1)}, u32[]{:S(2)}, u32[]{:S(2)}) collective-permute-start(bf16[72,3456]{1,0:T(8,128)(2,1)S(1)} %collective-permute-done.8), channel_id=1, source_target_pairs={{0,2},{2,4},{4,6},{6,8},{8,10},{10,12},{12,14},{14,16},{16,18},{18... | collective-permute-start | bytes 1493000 | tf_op jit(solution)/shard_map/ppermute | solution.py:24
  231.0 16.6 %collective-permute-start.11 = (bf16[72,3456]{1,0:T(8,128)(2,1)S(1)}, bf16[72,3456]{1,0:T(8,128)(2,1)S(1)}, u32[]{:S(2)}, u32[]{:S(2)}) collective-permute-start(bf16[72,3456]{1,0:T(8,128)(2,1)S(1)} %collective-permute-done.9), channel_id=1, source_target_pairs={{0,30},{2,0},{4,2},{6,4},{8,6},{10,8},{12,10},{14,12},{16,14},{18,... | collective-permute-start | bytes 1493000 | tf_op jit(solution)/shard_map/ppermute | solution.py:31
  236.7 31.1 %collective-permute-start.12 = (bf16[72,3456]{1,0:T(8,128)(2,1)S(1)}, bf16[72,3456]{1,0:T(8,128)(2,1)S(1)}, u32[]{:S(2)}, u32[]{:S(2)}) collective-permute-start(bf16[72,3456]{1,0:T(8,128)(2,1)S(1)} %collective-permute-done.10), channel_id=1, source_target_pairs={{0,2},{2,4},{4,6},{6,8},{8,10},{10,12},{12,14},{14,16},{16,18},{18... | collective-permute-start | bytes 1493000 | tf_op jit(solution)/shard_map/ppermute | solution.py:24
  247.5 21.6 %collective-permute-start.13 = (bf16[72,3456]{1,0:T(8,128)(2,1)S(1)}, bf16[72,3456]{1,0:T(8,128)(2,1)S(1)}, u32[]{:S(2)}, u32[]{:S(2)}) collective-permute-start(bf16[72,3456]{1,0:T(8,128)(2,1)S(1)} %collective-permute-done.11), channel_id=1, source_target_pairs={{0,30},{2,0},{4,2},{6,4},{8,6},{10,8},{12,10},{14,12},{16,14},{18,... | collective-permute-start | bytes 1493000 | tf_op jit(solution)/shard_map/ppermute | solution.py:31
  267.7 11.5 %collective-permute-start.14 = (bf16[72,3456]{1,0:T(8,128)(2,1)S(1)}, bf16[72,3456]{1,0:T(8,128)(2,1)S(1)}, u32[]{:S(2)}, u32[]{:S(2)}) collective-permute-start(bf16[72,3456]{1,0:T(8,128)(2,1)S(1)} %collective-permute-done.12), channel_id=1, source_target_pairs={{0,2},{2,4},{4,6},{6,8},{8,10},{10,12},{12,14},{14,16},{16,18},{18... | collective-permute-start | bytes 1493000 | tf_op jit(solution)/shard_map/ppermute | solution.py:24
  438.2 307.9 %reduce-scatter.13.cloned.1.call-start = ((), (), s32[]{:S(2)}) async-start(), calls=%async_computation.11 | async-start | bytes 8460288
  631.5 224.1 %reduce-scatter.9.cloned.1.call-start = ((), (), s32[]{:S(2)}) async-start(), calls=%async_computation.8 | async-start | bytes 11280384 | tf_op jit(solution)/shard_map/reduce_scatter | solution.py:290
  641.2 338.8 %reduce-scatter.11.cloned.1.call-start = ((), (), s32[]{:S(2)}) async-start(), calls=%async_computation.9 | async-start | bytes 11280384 | tf_op jit(solution)/shard_map/reduce_scatter | solution.py:231
  652.6 404.3 %all-reduce.20.cloned.1.call-start = ((), (), s32[]{:S(2)}) async-start(), calls=%async_computation.13 | async-start | bytes 3981312 | tf_op jit(solution)/shard_map/psum | solution.py:319
  (23 other events, 410.7 us)
Sparse Core Ops, SparseCore 0:
  81.6 87.4 all-reduce.17
  171.3 58.9 all-gather.6
  232.6 95.8 all-gather.8
  330.6 85.7 all-gather.10
  418.4 69.8 all-gather.12
  492.0 61.6 reduce-scatter.14
  631.6 99.4 reduce-scatter.12
  735.1 120.3 reduce-scatter.8
  859.6 120.2 reduce-scatter.10
  982.3 72.9 all-reduce.19
